TPU v7x, 256 devices: a whole 4x4x8 slice. The times are simulated.
256 devices in a mesh: node: 64 (over x_hi, z, y), col: 4 (over x_lo, core).
Axes of the slice: x: 4 (x_hi: 2, x_lo: 2; x = x_hi * 2 + x_lo), y: 4, z: 8, core: 2. Of those that a mesh axis runs over, the one named last changes fastest.
Arguments:
- panel: bfloat16 [311296, 256], P('node', 'col'), may hold values from -6 to 6
- basis: bfloat16 [311296, 2048], P('node', 'col'), may hold values from -0.03125 to 0.03125
- g_blocks: bfloat16 [2432, 3, 128, 128], P('node'), may hold values from -0.3125 to 0.3125
- c_blocks: bfloat16 [2432, 3, 128, 128], P('node'), may hold values from -0.3125 to 0.3125
- block_cols: int32 [2432, 3], P('node'), may hold values from 0 to 2431, as said below
Outputs:
- reduced_g: float32 [2048, 256], P(('col', 'node'))
- reduced_c: float32 [2048, 256], P(('col', 'node'))
Inputs may be any that keep to these rules, and one draw needn't show every extreme that they name: `block_cols`: block row i names block columns within 4 of i: the first is i itself, and one lies exactly 4 away wherever that stays inside the grid.
All inputs are finite; a program needn't handle non-finite values.
Results may differ from a plain program's by a relative error of at most 0.0029.
Values may be sent and summed in bfloat16 or wider, within the bound.
A program may use at most 64 MiB of HBM per device.

v0:
```python
import jax
import jax.numpy as jnp
from jax import lax
from jax.sharding import PartitionSpec as P

BS = 128
HB = 4


def with_halo(block, sides, width):
    for axis, dim in sides:
        count = lax.axis_size(axis)
        forward = [(i, i + 1) for i in range(count - 1)]
        backward = [(target, source) for source, target in forward]
        low = lax.ppermute(
            lax.slice_in_dim(block, block.shape[dim] - width, None, axis=dim), axis, forward
        )
        high = lax.ppermute(lax.slice_in_dim(block, 0, width, axis=dim), axis, backward)
        block = jnp.concatenate([low, block, high], axis=dim)
    return block


def spread_product(extended, blocks_g, blocks_c, local_ids):
    rows_dev = blocks_g.shape[0]
    block_size = blocks_g.shape[2]
    columns = extended.shape[1]
    block_tiles = extended.reshape(-1, block_size, columns)
    nearby = block_tiles[local_ids]
    prod_g = jnp.einsum("rsab,rsbk->rak", blocks_g, nearby, preferred_element_type=jnp.float32)
    prod_c = jnp.einsum("rsab,rsbk->rak", blocks_c, nearby, preferred_element_type=jnp.float32)
    stacked = jnp.stack([prod_g, prod_c], 2).astype(jnp.bfloat16)
    return stacked.reshape(rows_dev * block_size, 2, columns)


def body(panel, basis, g_blocks, c_blocks, block_cols):
    blocks_dev = block_cols.shape[0]
    offset = lax.axis_index("node") * blocks_dev - HB
    local_ids = block_cols - offset
    extended = with_halo(panel, (("node", 0),), HB * BS)
    stacked = lax.all_gather(
        spread_product(extended, g_blocks, c_blocks, local_ids), "col", axis=2, tiled=True
    )
    combined = stacked.reshape(stacked.shape[0], -1)
    reduced = lax.psum_scatter(
        lax.dot_general(
            basis, combined, (((0,), (0,)), ((), ())), preferred_element_type=jnp.float32
        ),
        "node",
        scatter_dimension=0,
        tiled=True,
    )
    half_cols = combined.shape[1] // 2
    return (reduced[:, :half_cols], reduced[:, half_cols:])


def solution(mesh):
    in_specs = (
        P("node", "col"),
        P("node", "col"),
        P("node", None, None, None),
        P("node", None, None, None),
        P("node", None),
    )
    out_specs = (P(("col", "node"), None), P(("col", "node"), None))
    return jax.shard_map(body, mesh=mesh, in_specs=in_specs, out_specs=out_specs, check_vma=False)
```

profile of v0, /device:TPU:2, one launch (start us, length us, event | category | flops | bytes accessed | tf_op | source)
XLA Modules:
  0.0 468.9 jit_solution(15038887618581699142)
XLA Ops:
  7.2 0.0 all-gather.2.cloned.1.call-start
  7.2 0.9 fusion.4
  8.1 3.5 collective-permute-start
  11.6 1.3 collective-permute-start.1
  12.9 0.7 compare_select_fusion
  13.6 0.1 copy.17
  13.7 0.1 reshape.21
  13.8 0.0 collective-permute-done
  13.8 3.9 collective-permute-done.1
  17.7 1.3 copy_bitcast_fusion
  19.0 0.9 gather_fusion
  19.9 0.0 copy-start
  20.0 4.0 fusion.3
  23.9 0.0 copy-done
  23.9 1.8 fusion.2
  25.7 0.4 copy.20
  26.1 0.3 stack.10
  26.5 0.4 copy.19
  26.9 0.3 stack.9
  27.3 1.2 pad_maximum_fusion
  28.4 0.0 all-gather.2.cloned.1.call-update
  28.5 0.0 reduce-scatter.4.cloned.1.call-start
  28.5 58.7 %all-gather.2.cloned.1.call-done = bf16[4864,2,256]{0,2,1:T(8,128)(2,1)} async-done(((bf16[4864,2,64]{0,2,1:T(8,128)(2,1)}), bf16[4864,2,256]{0,2,1:T(8,128)(2,1)}) %all-gather.2.cloned.1.call-update) | async-done | bytes 4980752 | tf_op jit(solution)/shard_map/all_gather | solution.py:40
  87.3 6.2 %convolution_bitcast_fusion.2 = f32[512,512]{0,1:T(8,128)S(1)} fusion(bf16[4864,512]{0,1:T(8,128)(2,1)} %bitcast.40, bf16[4864,512]{1,0:T(8,128)(2,1)} %param.6), kind=kOutput, calls=%fused_computation.3 | convolution fusion | flops 2550136832 | bytes 11010048 | tf_op jit(solution)/shard_map/dot_general | solution.py:45
  93.5 1.3 copy.25
  94.8 0.0 reduce-scatter.4.cloned.1.call-update
  94.8 365.9 %reduce-scatter.4.cloned.1.call-done = f32[8,512]{1,0:T(8,128)} async-done(((f32[512,512]{1,0:T(8,128)}), f32[8,512]{1,0:T(8,128)}) %reduce-scatter.4.cloned.1.call-update) | async-done | bytes 16400
  460.7 1.3 fusion.5
  (1 shorter events, 0.0 us)
Async XLA Ops:
  7.2 80.1 %all-gather.2.cloned.1.call-start = ((), (), s32[]{:S(2)}) async-start(), calls=%async_computation.1 | async-start | bytes 6225920 | tf_op jit(solution)/shard_map/all_gather | solution.py:40
  8.1 5.7 %collective-permute-start = (bf16[512,64]{0,1:T(8,128)(2,1)S(1)}, bf16[512,64]{0,1:T(8,128)(2,1)S(1)}, u32[]{:S(2)}, u32[]{:S(2)}) collective-permute-start(bf16[512,64]{0,1:T(8,128)(2,1)S(1)} %get-tuple-element.8), channel_id=1, source_target_pairs={{0,4},{4,8},{8,12},{12,16},{16,20},{20,24},{24,28},{28,32},{32,36}... | collective-permute-start | bytes 196616 | tf_op jit(solution)/shard_map/ppermute | solution.py:15
  11.6 6.2 %collective-permute-start.1 = (bf16[512,64]{0,1:T(8,128)(2,1)S(1)}, bf16[512,64]{0,1:T(8,128)(2,1)S(1)}, u32[]{:S(2)}, u32[]{:S(2)}) collective-permute-start(bf16[512,64]{0,1:T(8,128)(2,1)S(1)} %get-tuple-element.9), channel_id=1, source_target_pairs={{4,0},{8,4},{12,8},{16,12},{20,16},{24,20},{28,24},{32,28},{36,32}... | collective-permute-start | bytes 196616 | tf_op jit(solution)/shard_map/ppermute | solution.py:18
  19.9 4.0 copy-start
  28.5 432.2 %reduce-scatter.4.cloned.1.call-start = ((), (), s32[]{:S(2)}) async-start(), calls=%async_computation.2 | async-start | bytes 1064960
Sparse Core Ops, SparseCore 0:
  28.6 58.6 all-gather.1
  94.9 365.7 reduce-scatter.3
where the time goes:
time: 469 us
  waiting for transfers between devices  429 us (91%)
  between operations  14.2 us (3%)
  matrix products  11.9 us (3%)
  local copies, waits for them, and re-layouts  6.16 us (1%)
  starting transfers between devices  4.85 us (1%)
    unnamed x3, waiting for transfers between devices  366 us
    all_gather x1, waiting for transfers between devices, body(): lax.all_gather(spread_product(extended, g_blocks, c_blocks, local_ids), '...  58.7 us
  transfers between devices with their start and end apart: 4, of which 3 were waited for; matrix products, arithmetic and copies ran while one was open for 0% of the time, Pallas kernels for 0%

commit v1 on v0

v1 whole, which is shorter than its diff:
```python
import functools

import jax
import jax.numpy as jnp
from jax import lax
from jax.experimental import pallas as pl
from jax.experimental.pallas import tpu as pltpu
from jax.sharding import PartitionSpec as P

BS = 128
HB = 4
MESH = pl.DeviceIdType.MESH
F32, BF16 = jnp.float32, jnp.bfloat16
INNER = (4, 13, 22, 29, 34)
ROW_UNROLL = 2


def span(first, last):
    return pl.ds(first * BS, (last - first) * BS)


def kernel(
    nodes, xt, basis, gb, cb, bc, outg, outc,
    xl, xr, wl, w0, w1, w2, w3, gv, cv, bv, yt, acc, stage, land,
    lsem, ssem, rsem, sum_send, sum_recv,
):
    nb = gb.shape[0]
    width = xt.shape[0]
    node, col = lax.axis_index("node"), lax.axis_index("col")
    core, x_lo = lax.rem(col, 2), col // 2
    y, z, x_hi = lax.rem(node, 4), lax.rem(node // 4, 8), node // 32
    above = (lax.rem(node + 1, nodes), col)
    below = (lax.rem(node + nodes - 1, nodes), col)
    across = (node, lax.rem(col + 2, 4))
    beside = (node, col + 1 - 2 * core)
    mine = pl.ds(pl.multiple_of(core * width, width), width)

    loads = [pltpu.make_async_copy(xt, xl.at[mine, span(HB, HB + nb)], lsem.at[0])]
    half = nb // 2
    for k, (src, dst) in enumerate(((gb, gv), (cb, cv))):
        for part in range(2):
            rows = pl.ds(part * half, half)
            loads.append(pltpu.make_async_copy(src.at[rows], dst.at[rows], lsem.at[1 + 2 * part + k]))
    loads.append(pltpu.make_async_copy(basis, bv, lsem.at[5]))
    for load in (loads[0], loads[1], loads[3], loads[2], loads[4], loads[5]):
        load.start()

    barrier = pltpu.get_barrier_semaphore()

    def greet(k, carry):
        pl.semaphore_signal(barrier, inc=1, device_id=(lax.rem(node + k, nodes), col), device_id_type=MESH)
        return carry

    pl.semaphore_signal(barrier, inc=1, device_id=across, device_id_type=MESH)
    pl.semaphore_signal(barrier, inc=1, device_id=beside, device_id_type=MESH)
    lax.fori_loop(1, nodes, greet, 0)
    pl.semaphore_wait(barrier, nodes + 1)

    made = []

    def remote(src, dst, device):
        k = len(made)
        made.append(
            pltpu.make_async_remote_copy(
                src_ref=src, dst_ref=dst, send_sem=ssem.at[k], recv_sem=rsem.at[k],
                device_id=device, device_id_type=MESH,
            )
        )
        return made[-1]

    chunks = [(0, HB), (nb - HB, nb)] + list(zip(INNER[:-1], INNER[1:]))
    lo, hi = span(0, HB), span(nb - HB, nb)
    halo_lo, halo_hi = span(0, HB), span(nb + HB, nb + 2 * HB)

    cross = [remote(xt.at[:, span(a, b)], xr.at[mine, span(a + HB, b + HB)], across) for a, b in chunks]
    pass_on = [
        remote(xr.at[mine, span(a + HB, b + HB)], xr.at[mine, span(a + HB, b + HB)], beside) for a, b in chunks
    ]
    own_up = remote(xt.at[:, hi], xl.at[mine, halo_lo], above)
    own_down = remote(xt.at[:, lo], xl.at[mine, halo_hi], below)
    own_body = remote(xt, xl.at[mine, span(HB, HB + nb)], beside)
    own_lo = remote(xl.at[mine, halo_lo], xl.at[mine, halo_lo], beside)
    own_hi = remote(xl.at[mine, halo_hi], xl.at[mine, halo_hi], beside)
    far_up = remote(xr.at[mine, span(nb, nb + HB)], xr.at[mine, halo_lo], above)
    far_down = remote(xr.at[mine, span(HB, 2 * HB)], xr.at[mine, halo_hi], below)
    far_lo = remote(xr.at[mine, halo_lo], xr.at[mine, halo_lo], beside)
    far_hi = remote(xr.at[mine, halo_hi], xr.at[mine, halo_hi], beside)

    for copy in (cross[0], cross[1], own_up, own_down, *cross[2:], own_body):
        copy.start()

    def fill(window, slices, shift):
        for b in range(window.shape[0]):
            window[b] = slices[:, span(b + shift, b + shift + 1)]

    def products(window, first, last, shift):
        def tile(s, i):
            return window[jnp.clip(bc[s, i] - (node * nb - HB + shift), 0, window.shape[0] - 1)]

        def row(i):
            tiles = [tile(s, i) for s in range(3)]
            rhs = jnp.concatenate(
                [jnp.concatenate([m[i, s] for s in range(3)], axis=1) for m in (gv, cv)], axis=0
            )
            made_rows = lax.dot_general(
                jnp.concatenate(tiles, axis=1), rhs, (((1,), (1,)), ((), ())), preferred_element_type=F32
            ).astype(BF16)
            at = pl.ds(pl.multiple_of(i * BS, BS), BS)
            yt[: 2 * width, at] = made_rows[:, :BS]
            yt[2 * width :, at] = made_rows[:, BS:]

        count = last - first
        steps = count // ROW_UNROLL

        def several(k, carry):
            for u in range(ROW_UNROLL):
                row(first + k * ROW_UNROLL + u)
            return carry

        lax.fori_loop(0, steps, several, 0)
        for i in range(first + steps * ROW_UNROLL, last):
            row(i)

    def project(first, last, fresh):
        rows = span(first, last)
        part = jnp.dot(yt[:, rows], bv[rows, :], preferred_element_type=F32)
        acc[...] = part if fresh else acc[...] + part

    def place(k):
        to_x = lax.rem(x_hi + 1 - k // 32, 2)
        to_z = lax.rem(z + lax.rem(k // 4, 8) + 4, 8)
        to_y = lax.rem(y + lax.rem(k, 4) + 2, 4)
        return (to_x * 8 + to_z) * 4 + to_y

    own_k = 32 + 4 * 4 + 2

    def scatter(which):
        for s in range(acc.shape[1] // BS):
            turned = acc[:, s * BS : (s + 1) * BS].T.astype(BF16)
            stage[which, s * 16 : (s + 1) * 16] = turned.reshape(16, 8, acc.shape[0])

        def send(slot, k):
            to = place(k)
            pltpu.make_async_remote_copy(
                src_ref=stage.at[which, to], dst_ref=land.at[which, slot],
                send_sem=sum_send.at[which], recv_sem=sum_recv.at[which],
                device_id=(to, col), device_id_type=MESH,
            ).start()

        def early(k, carry):
            send(k, k)
            return carry

        def late(k, carry):
            send(k - 1, k)
            return carry

        lax.fori_loop(0, own_k, early, 0)
        lax.fori_loop(own_k + 1, nodes, late, 0)

    def all_sums(which):
        return pltpu.make_async_remote_copy(
            src_ref=stage.at[which, pl.ds(0, nodes - 1)], dst_ref=land.at[which, pl.ds(0, nodes - 1)],
            send_sem=sum_send.at[which], recv_sem=sum_recv.at[which],
            device_id=across, device_id_type=MESH,
        )

    def gather_sums(which, at):
        all_sums(which).wait_recv()
        total = stage[which, node].astype(F32)
        for k in range(nodes - 1):
            total = total + land[which, k].astype(F32)
        outg[:, at] = total[:, : 2 * width]
        outc[:, at] = total[:, 2 * width :]

    own_up.wait_recv()
    own_lo.start()
    own_down.wait_recv()
    own_hi.start()
    cross[0].wait_recv()
    pass_on[0].start()
    far_down.start()
    cross[1].wait_recv()
    pass_on[1].start()
    far_up.start()
    loads[0].wait()
    own_body.wait_recv()
    own_lo.wait_recv()
    own_hi.wait_recv()

    loads[1].wait()
    loads[3].wait()
    fill(wl, xl, 0)
    products(wl, 0, half, 0)
    cross[2].wait_recv()
    pass_on[2].start()
    far_up.wait_recv()
    far_lo.start()
    far_down.wait_recv()
    far_hi.start()
    loads[2].wait()
    loads[4].wait()
    products(wl, half, nb, 0)
    loads[5].wait()
    project(0, half, True)
    cross[3].wait_recv()
    pass_on[3].start()
    project(half, nb, False)
    scatter(0)

    far_lo.wait_recv()
    far_hi.wait_recv()
    pass_on[0].wait_recv()
    pass_on[1].wait_recv()
    ends = [b - HB for b in INNER[1:-1]] + [nb]
    starts = [0] + ends[:-1]
    for p, (window, a, b) in enumerate(zip((w0, w1, w2, w3), starts, ends)):
        if p >= 2:
            cross[2 + p].wait_recv()
            pass_on[2 + p].start()
        pass_on[2 + p].wait_recv()
        fill(window, xr, a)
        products(window, a, b, a)
        project(a, b, p == 0)
    scatter(1)

    near_at = pl.ds(pl.multiple_of(x_lo * 2 * width, 2 * width), 2 * width)
    far_at = pl.ds(pl.multiple_of((1 - x_lo) * 2 * width, 2 * width), 2 * width)
    gather_sums(0, near_at)
    gather_sums(1, far_at)
    for copy in made:
        copy.wait_send()
    for which in range(2):
        all_sums(which).wait_send()


def body(panel, basis, g_blocks, c_blocks, block_cols):
    nodes = lax.axis_size("node")
    nb = g_blocks.shape[0]
    width, states = panel.shape[1], basis.shape[1]
    ext = (nb + 2 * HB) * BS
    ends = [b - HB for b in INNER[1:-1]] + [nb]
    starts = [0] + ends[:-1]
    any_spec = pl.BlockSpec(memory_space=pl.ANY)
    vmem_spec = pl.BlockSpec(memory_space=pltpu.VMEM)
    reduced = jax.ShapeDtypeStruct((states // nodes, 4 * width), F32)
    return pl.pallas_call(
        functools.partial(kernel, nodes),
        out_shape=(reduced, reduced),
        in_specs=[any_spec] * 4 + [pl.BlockSpec(memory_space=pltpu.SMEM)],
        out_specs=(vmem_spec, vmem_spec),
        scratch_shapes=[
            pltpu.VMEM((2 * width, ext), BF16),
            pltpu.VMEM((2 * width, ext), BF16),
            *[pltpu.VMEM((b - a + 2 * HB, 2 * width, BS), BF16) for a, b in zip([0] + starts, [nb] + ends)],
            pltpu.VMEM(g_blocks.shape, BF16),
            pltpu.VMEM(c_blocks.shape, BF16),
            pltpu.VMEM(basis.shape, BF16),
            pltpu.VMEM((4 * width, nb * BS), BF16),
            pltpu.VMEM((4 * width, states), F32),
            pltpu.VMEM((2, nodes, states // nodes, 4 * width), BF16),
            pltpu.VMEM((2, nodes, states // nodes, 4 * width), BF16),
            pltpu.SemaphoreType.DMA((6,)),
            pltpu.SemaphoreType.DMA((24,)),
            pltpu.SemaphoreType.DMA((24,)),
            pltpu.SemaphoreType.DMA((2,)),
            pltpu.SemaphoreType.DMA((2,)),
        ],
        compiler_params=pltpu.CompilerParams(
            collective_id=0, has_side_effects=True, vmem_limit_bytes=61 << 20
        ),
        name="project",
    )(panel.T, basis, g_blocks, c_blocks, block_cols.T)


def solution(mesh):
    in_specs = (
        P("node", "col"),
        P("node", "col"),
        P("node", None, None, None),
        P("node", None, None, None),
        P("node", None),
    )
    out_specs = (P(("col", "node"), None), P(("col", "node"), None))
    return jax.shard_map(body, mesh=mesh, in_specs=in_specs, out_specs=out_specs, check_vma=False)
```

time: 469 us -> 52 us (0.11)
  the two profiles are of different devices: /device:TPU:2 before, /device:TPU:1 now
where the time goes in v1:
time: 52 us; the launch traced here: 51.7 us
  Pallas kernels  48.5 us (93%)
  local copies, waits for them, and re-layouts  2.59 us (5%)
  between operations  0.64 us (1%)
    pallas_call x1, Pallas kernels, body(): pl.pallas_call(functools.partial(kernel, nodes), out_shape=(reduced, redu...  48.5 us
    unnamed x2, local copies, waits for them, and re-layouts  2.59 us

profile of v1, /device:TPU:1, one launch (start us, length us, event | category | flops | bytes accessed | tf_op | source)
XLA Modules:
  0.0 51.7 jit_solution(12786328886266231172)
XLA Ops:
  0.6 48.5 %project.1 = (f32[8,256]{1,0:T(8,128)}, f32[8,256]{1,0:T(8,128)}) custom-call(bf16[64,4864]{1,0:T(8,128)(2,1)} %bitcast.2, bf16[4864,512]{1,0:T(8,128)(2,1)} %basis.1, bf16[38,3,128,128]{3,2,1,0:T(8,128)(2,1)} %gb.1, bf16[38,3,128,128]{3,2,1,0:T(8,128)(2,1)} %cb.1, s32[3,38]{1,0:T(4,128)} %bitcast.3), custom_call_target="tpu_custom_call" | custom-call | tf_op jit(solution)/shard_map/project/pallas_call | solution.py:247
  49.1 1.3 %copy.9 = f32[8,256]{1,0:T(8,128)} copy(f32[8,256]{1,0:T(8,128)} %get-tuple-element.4) | data formatting | bytes 16384
  50.4 1.3 %copy.10 = f32[8,256]{1,0:T(8,128)} copy(f32[8,256]{1,0:T(8,128)} %get-tuple-element.5) | data formatting | bytes 16384

commit v2 on v1

--- a/solution.py
+++ b/solution.py
@@ -11,8 +11,8 @@
 HB = 4
 MESH = pl.DeviceIdType.MESH
 F32, BF16 = jnp.float32, jnp.bfloat16
-INNER = (4, 13, 22, 29, 34)
-ROW_UNROLL = 2
+INNER = (4, 13, 22, 32, 34)
+ROW_UNROLL = 15
 
 
 def span(first, last):
@@ -20,8 +20,8 @@
 
 
 def kernel(
-    nodes, xt, basis, gb, cb, bc, outg, outc,
-    xl, xr, wl, w0, w1, w2, w3, gv, cv, bv, yt, acc, stage, land,
+    nodes, xt, basis, gb, cb, bc, out,
+    xl, xr, wi, we, wf, w0, w1, w2, w3, gv, cv, bv, yt, acc, stage, land,
     lsem, ssem, rsem, sum_send, sum_recv,
 ):
     nb = gb.shape[0]
@@ -33,6 +33,7 @@
     below = (lax.rem(node + nodes - 1, nodes), col)
     across = (node, lax.rem(col + 2, 4))
     beside = (node, col + 1 - 2 * core)
+    diagonal = (node, lax.rem(col + 2, 4) + 1 - 2 * core)
     mine = pl.ds(pl.multiple_of(core * width, width), width)
 
     loads = [pltpu.make_async_copy(xt, xl.at[mine, span(HB, HB + nb)], lsem.at[0])]
@@ -51,10 +52,10 @@
         pl.semaphore_signal(barrier, inc=1, device_id=(lax.rem(node + k, nodes), col), device_id_type=MESH)
         return carry
 
-    pl.semaphore_signal(barrier, inc=1, device_id=across, device_id_type=MESH)
-    pl.semaphore_signal(barrier, inc=1, device_id=beside, device_id_type=MESH)
+    for near in (across, beside, diagonal):
+        pl.semaphore_signal(barrier, inc=1, device_id=near, device_id_type=MESH)
     lax.fori_loop(1, nodes, greet, 0)
-    pl.semaphore_wait(barrier, nodes + 1)
+    pl.semaphore_wait(barrier, nodes + 2)
 
     made = []
 
@@ -74,8 +75,10 @@
 
     cross = [remote(xt.at[:, span(a, b)], xr.at[mine, span(a + HB, b + HB)], across) for a, b in chunks]
     pass_on = [
-        remote(xr.at[mine, span(a + HB, b + HB)], xr.at[mine, span(a + HB, b + HB)], beside) for a, b in chunks
+        remote(xr.at[mine, span(a + HB, b + HB)], xr.at[mine, span(a + HB, b + HB)], beside) for a, b in chunks[:-1]
     ]
+    last = span(*chunks[-1])
+    cross_both = remote(xt.at[:, last], xr.at[mine, span(INNER[-2] + HB, INNER[-1] + HB)], diagonal)
     own_up = remote(xt.at[:, hi], xl.at[mine, halo_lo], above)
     own_down = remote(xt.at[:, lo], xl.at[mine, halo_hi], below)
     own_body = remote(xt, xl.at[mine, span(HB, HB + nb)], beside)
@@ -86,7 +89,7 @@
     far_lo = remote(xr.at[mine, halo_lo], xr.at[mine, halo_lo], beside)
     far_hi = remote(xr.at[mine, halo_hi], xr.at[mine, halo_hi], beside)
 
-    for copy in (cross[0], cross[1], own_up, own_down, *cross[2:], own_body):
+    for copy in (cross[0], cross[1], own_up, own_down, own_body, *cross[2:], cross_both):
         copy.start()
 
     def fill(window, slices, shift):
@@ -110,14 +113,15 @@
             yt[2 * width :, at] = made_rows[:, BS:]
 
         count = last - first
-        steps = count // ROW_UNROLL
+        steps = count // ROW_UNROLL if count > ROW_UNROLL else 0
 
         def several(k, carry):
             for u in range(ROW_UNROLL):
                 row(first + k * ROW_UNROLL + u)
             return carry
 
-        lax.fori_loop(0, steps, several, 0)
+        if steps:
+            lax.fori_loop(0, steps, several, 0)
         for i in range(first + steps * ROW_UNROLL, last):
             row(i)
 
@@ -126,37 +130,21 @@
         part = jnp.dot(yt[:, rows], bv[rows, :], preferred_element_type=F32)
         acc[...] = part if fresh else acc[...] + part
 
-    def place(k):
-        to_x = lax.rem(x_hi + 1 - k // 32, 2)
-        to_z = lax.rem(z + lax.rem(k // 4, 8) + 4, 8)
-        to_y = lax.rem(y + lax.rem(k, 4) + 2, 4)
-        return (to_x * 8 + to_z) * 4 + to_y
-
-    own_k = 32 + 4 * 4 + 2
+    to_x = [lax.rem(x_hi + d, 2) * 32 for d in (1, 0)]
+    to_z = [lax.rem(z + d, 8) * 4 for d in (4, 3, 5, 2, 6, 1, 7, 0)]
+    to_y = [lax.rem(y + d, 4) for d in (2, 1, 3, 0)]
+    owners = [tx + tz + ty for tz in to_z for tx in to_x for ty in to_y][:-1]
 
     def scatter(which):
         for s in range(acc.shape[1] // BS):
             turned = acc[:, s * BS : (s + 1) * BS].T.astype(BF16)
             stage[which, s * 16 : (s + 1) * 16] = turned.reshape(16, 8, acc.shape[0])
-
-        def send(slot, k):
-            to = place(k)
+        for slot, to in enumerate(owners):
             pltpu.make_async_remote_copy(
                 src_ref=stage.at[which, to], dst_ref=land.at[which, slot],
                 send_sem=sum_send.at[which], recv_sem=sum_recv.at[which],
                 device_id=(to, col), device_id_type=MESH,
             ).start()
-
-        def early(k, carry):
-            send(k, k)
-            return carry
-
-        def late(k, carry):
-            send(k - 1, k)
-            return carry
-
-        lax.fori_loop(0, own_k, early, 0)
-        lax.fori_loop(own_k + 1, nodes, late, 0)
 
     def all_sums(which):
         return pltpu.make_async_remote_copy(
@@ -170,58 +158,62 @@
         total = stage[which, node].astype(F32)
         for k in range(nodes - 1):
             total = total + land[which, k].astype(F32)
-        outg[:, at] = total[:, : 2 * width]
-        outc[:, at] = total[:, 2 * width :]
+        out[0, :, at] = total[:, : 2 * width]
+        out[1, :, at] = total[:, 2 * width :]
 
     own_up.wait_recv()
     own_lo.start()
     own_down.wait_recv()
     own_hi.start()
+
+    loads[0].wait()
+    own_body.wait_recv()
+    fill(wi, xl, HB)
+    for load in loads[1:5]:
+        load.wait()
+    products(wi, HB, nb - HB, HB)
     cross[0].wait_recv()
     pass_on[0].start()
     far_down.start()
     cross[1].wait_recv()
     pass_on[1].start()
     far_up.start()
-    loads[0].wait()
-    own_body.wait_recv()
     own_lo.wait_recv()
+    fill(we, xl, 0)
+    products(we, 0, HB, 0)
     own_hi.wait_recv()
-
-    loads[1].wait()
-    loads[3].wait()
-    fill(wl, xl, 0)
-    products(wl, 0, half, 0)
+    fill(wf, xl, nb - HB)
+    products(wf, nb - HB, nb, nb - HB)
     cross[2].wait_recv()
     pass_on[2].start()
+    loads[5].wait()
+    project(0, nb, True)
     far_up.wait_recv()
     far_lo.start()
     far_down.wait_recv()
     far_hi.start()
-    loads[2].wait()
-    loads[4].wait()
-    products(wl, half, nb, 0)
-    loads[5].wait()
-    project(0, half, True)
     cross[3].wait_recv()
     pass_on[3].start()
-    project(half, nb, False)
     scatter(0)
 
-    far_lo.wait_recv()
-    far_hi.wait_recv()
-    pass_on[0].wait_recv()
-    pass_on[1].wait_recv()
     ends = [b - HB for b in INNER[1:-1]] + [nb]
     starts = [0] + ends[:-1]
+    far_lo.wait_recv()
+    pass_on[0].wait_recv()
     for p, (window, a, b) in enumerate(zip((w0, w1, w2, w3), starts, ends)):
-        if p >= 2:
-            cross[2 + p].wait_recv()
-            pass_on[2 + p].start()
-        pass_on[2 + p].wait_recv()
+        if p < 3:
+            pass_on[2 + p].wait_recv()
+        else:
+            far_hi.wait_recv()
+            pass_on[1].wait_recv()
+            cross[5].wait_recv()
+            cross_both.wait_recv()
         fill(window, xr, a)
         products(window, a, b, a)
         project(a, b, p == 0)
+        if p == 1:
+            cross[4].wait_recv()
+            pass_on[4].start()
     scatter(1)
 
     near_at = pl.ds(pl.multiple_of(x_lo * 2 * width, 2 * width), 2 * width)
@@ -243,16 +235,16 @@
     starts = [0] + ends[:-1]
     any_spec = pl.BlockSpec(memory_space=pl.ANY)
     vmem_spec = pl.BlockSpec(memory_space=pltpu.VMEM)
-    reduced = jax.ShapeDtypeStruct((states // nodes, 4 * width), F32)
-    return pl.pallas_call(
+    windows = [(HB, nb - HB), (0, HB), (nb - HB, nb), *zip(starts, ends)]
+    reduced = pl.pallas_call(
         functools.partial(kernel, nodes),
-        out_shape=(reduced, reduced),
+        out_shape=jax.ShapeDtypeStruct((2, states // nodes, 4 * width), F32),
         in_specs=[any_spec] * 4 + [pl.BlockSpec(memory_space=pltpu.SMEM)],
-        out_specs=(vmem_spec, vmem_spec),
+        out_specs=vmem_spec,
         scratch_shapes=[
             pltpu.VMEM((2 * width, ext), BF16),
             pltpu.VMEM((2 * width, ext), BF16),
-            *[pltpu.VMEM((b - a + 2 * HB, 2 * width, BS), BF16) for a, b in zip([0] + starts, [nb] + ends)],
+            *[pltpu.VMEM((b - a + 2 * HB, 2 * width, BS), BF16) for a, b in windows],
             pltpu.VMEM(g_blocks.shape, BF16),
             pltpu.VMEM(c_blocks.shape, BF16),
             pltpu.VMEM(basis.shape, BF16),
@@ -271,6 +263,7 @@
         ),
         name="project",
     )(panel.T, basis, g_blocks, c_blocks, block_cols.T)
+    return reduced[0], reduced[1]
 
 
 def solution(mesh):

time: 52 us -> 47 us (0.904)
  Pallas kernels: 48.5 us -> 44.8 us
  local copies, waits for them, and re-layouts: 2.59 us -> 1.32 us
    pallas_call x1, Pallas kernels: 48.5 us -> 44.8 us  [body(): pl.pallas_call(functools.partial(kernel, nodes), out_shape=jax.ShapeDtype...]
    unnamed x2 -> x0, local copies, waits for them, and re-layouts: 2.59 us -> none
    squeeze x0 -> x1, local copies, waits for them, and re-layouts: none -> 1.32 us  [body(): return (reduced[0], reduced[1])]
where the time goes in v2:
time: 47 us; the launch traced here: 46.8 us
  Pallas kernels  44.8 us (95%)
  local copies, waits for them, and re-layouts  1.32 us (3%)
  between operations  0.64 us (1%)
    pallas_call x1, Pallas kernels, body(): pl.pallas_call(functools.partial(kernel, nodes), out_shape=jax.ShapeDtype...  44.8 us
    squeeze x1, local copies, waits for them, and re-layouts, body(): return (reduced[0], reduced[1])  1.32 us

profile of v2, /device:TPU:1, one launch (start us, length us, event | category | flops | bytes accessed | tf_op | source)
XLA Modules:
  0.0 46.8 jit_solution(16922446616701212450)
XLA Ops:
  0.6 44.8 %project.1 = f32[2,8,256]{2,1,0:T(8,128)} custom-call(bf16[64,4864]{1,0:T(8,128)(2,1)} %bitcast.6, bf16[4864,512]{1,0:T(8,128)(2,1)} %basis.1, bf16[38,3,128,128]{3,2,1,0:T(8,128)(2,1)} %gb.1, bf16[38,3,128,128]{3,2,1,0:T(8,128)(2,1)} %cb.1, s32[3,38]{1,0:T(4,128)} %bitcast.7), custom_call_target="tpu_custom_call" | custom-call | tf_op jit(solution)/shard_map/project/pallas_call | solution.py:239
  45.5 1.3 %slice_bitcast_fusion = (f32[8,256]{1,0:T(8,128)}, f32[8,256]{1,0:T(8,128)}) fusion(f32[2,8,256]{2,1,0:T(8,128)} %project.1), kind=kLoop, calls=%fused_computation | loop fusion | bytes 32768 | tf_op jit(solution)/shard_map/squeeze | solution.py:266

commit v3 on v2

v3 whole, which is shorter than its diff:
```python
import functools

import jax
import jax.numpy as jnp
from jax import lax
from jax.experimental import pallas as pl
from jax.experimental.pallas import tpu as pltpu
from jax.sharding import PartitionSpec as P

BS = 128
HB = 4
MESH = pl.DeviceIdType.MESH
F32, BF16 = jnp.float32, jnp.bfloat16
INNER = (4, 15, 26, 32, 34)
ROW_UNROLL = 15


def span(first, last):
    return pl.ds(first * BS, (last - first) * BS)


def kernel(
    nodes, xt, basis, gb, cb, bc, out,
    xl, xr, wi, we, wf, w0, w1, w2, w3, gv, cv, bv, yt, acc,
    stage, land, first, first_in, second, second_in, lsem, ssem, rsem, sum_send, sum_recv, part_send, part_recv, known,
):
    nb = gb.shape[0]
    width = xt.shape[0]
    node, col = lax.axis_index("node"), lax.axis_index("col")
    core, x_lo = lax.rem(col, 2), col // 2
    y, z, x_hi = lax.rem(node, 4), lax.rem(node // 4, 8), node // 32
    above = (lax.rem(node + 1, nodes), col)
    below = (lax.rem(node + nodes - 1, nodes), col)
    above_beside = (above[0], col + 1 - 2 * core)
    below_beside = (below[0], col + 1 - 2 * core)
    across = (node, lax.rem(col + 2, 4))
    beside = (node, col + 1 - 2 * core)
    diagonal = (node, lax.rem(col + 2, 4) + 1 - 2 * core)
    mine = pl.ds(pl.multiple_of(core * width, width), width)

    loads = [pltpu.make_async_copy(xt, xl.at[mine, span(HB, HB + nb)], lsem.at[0])]
    half = nb // 2
    for k, (src, dst) in enumerate(((gb, gv), (cb, cv))):
        for part in range(2):
            rows = pl.ds(part * half, half)
            loads.append(pltpu.make_async_copy(src.at[rows], dst.at[rows], lsem.at[1 + 2 * part + k]))
    loads.append(pltpu.make_async_copy(basis, bv, lsem.at[5]))
    for load in (loads[0], loads[1], loads[3], loads[2], loads[4], loads[5]):
        load.start()

    barrier = pltpu.get_barrier_semaphore()
    y_line = [(node - y + lax.rem(y + d, 4), col) for d in (1, 2, 3)]
    z_line = [((x_hi * 8 + lax.rem(z + d, 8)) * 4 + y, col) for d in range(1, 8)]
    near = [across, beside, diagonal, (lax.rem(node + nodes // 2, nodes), col)] + y_line + z_line

    def greet(device):
        pl.semaphore_signal(barrier, inc=1, device_id=device, device_id_type=MESH)

    for peer in near:
        greet(peer)
    for peer in (above, below, above_beside, below_beside):
        greet(peer)
    pl.semaphore_wait(barrier, len(near) + 4)

    def tell(r):
        for peer in (y_line, z_line)[r]:
            pl.semaphore_signal(known.at[r], inc=1, device_id=peer, device_id_type=MESH)

    def hear(r):
        pl.semaphore_wait(known.at[r], len((y_line, z_line)[r]))

    made = []

    def remote(src, dst, device):
        k = len(made)
        made.append(
            pltpu.make_async_remote_copy(
                src_ref=src, dst_ref=dst, send_sem=ssem.at[k], recv_sem=rsem.at[k],
                device_id=device, device_id_type=MESH,
            )
        )
        return made[-1]

    chunks = [(0, HB), (nb - HB, nb)] + list(zip(INNER[:-1], INNER[1:]))
    lo, hi = span(0, HB), span(nb - HB, nb)
    halo_lo, halo_hi = span(0, HB), span(nb + HB, nb + 2 * HB)

    cross = [remote(xt.at[:, span(a, b)], xr.at[mine, span(a + HB, b + HB)], across) for a, b in chunks]
    pass_on = [
        remote(xr.at[mine, span(a + HB, b + HB)], xr.at[mine, span(a + HB, b + HB)], beside) for a, b in chunks[:-1]
    ]
    last = span(*chunks[-1])
    cross_both = remote(xt.at[:, last], xr.at[mine, span(INNER[-2] + HB, INNER[-1] + HB)], diagonal)
    own_up = [remote(xt.at[:, hi], xl.at[mine, halo_lo], to) for to in (above, above_beside)]
    own_down = [remote(xt.at[:, lo], xl.at[mine, halo_hi], to) for to in (below, below_beside)]
    own_body = remote(xt, xl.at[mine, span(HB, HB + nb)], beside)
    far_up = [remote(xr.at[mine, span(nb, nb + HB)], xr.at[mine, halo_lo], to) for to in (above, above_beside)]
    far_down = [remote(xr.at[mine, span(HB, 2 * HB)], xr.at[mine, halo_hi], to) for to in (below, below_beside)]

    for copy in (cross[0], cross[1], own_body, *own_up, *own_down, *cross[2:], cross_both):
        copy.start()

    def fill(window, slices, shift):
        for b in range(window.shape[0]):
            window[b] = slices[:, span(b + shift, b + shift + 1)]

    def products(window, first, last, shift):
        def tile(s, i):
            return window[jnp.clip(bc[s, i] - (node * nb - HB + shift), 0, window.shape[0] - 1)]

        def row(i):
            tiles = [tile(s, i) for s in range(3)]
            rhs = jnp.concatenate(
                [jnp.concatenate([m[i, s] for s in range(3)], axis=1) for m in (gv, cv)], axis=0
            )
            made_rows = lax.dot_general(
                jnp.concatenate(tiles, axis=1), rhs, (((1,), (1,)), ((), ())), preferred_element_type=F32
            ).astype(BF16)
            at = pl.ds(pl.multiple_of(i * BS, BS), BS)
            yt[: 2 * width, at] = made_rows[:, :BS]
            yt[2 * width :, at] = made_rows[:, BS:]

        count = last - first
        steps = count // ROW_UNROLL if count > ROW_UNROLL else 0

        def several(k, carry):
            for u in range(ROW_UNROLL):
                row(first + k * ROW_UNROLL + u)
            return carry

        if steps:
            lax.fori_loop(0, steps, several, 0)
        for i in range(first + steps * ROW_UNROLL, last):
            row(i)

    def project(first, last, fresh):
        rows = span(first, last)
        part = jnp.dot(yt[:, rows], bv[rows, :], preferred_element_type=F32)
        acc[...] = part if fresh else acc[...] + part

    to_x = [lax.rem(x_hi + d, 2) * 32 for d in (1, 0)]
    to_z = [lax.rem(z + d, 8) * 4 for d in (4, 3, 5, 2, 6, 1, 7, 0)]
    to_y = [lax.rem(y + d, 4) for d in (2, 1, 3, 0)]
    owners = [tx + tz + ty for tz in to_z for tx in to_x for ty in to_y][:-1]

    along_y = [
        pltpu.make_async_remote_copy(
            src_ref=first.at[to], dst_ref=first_in.at[k], send_sem=part_send.at[k], recv_sem=part_recv.at[k],
            device_id=(node - y + to, col), device_id_type=MESH,
        )
        for k, to in enumerate(to_y[:3])
    ]
    lines = [tx // 4 + tz // 4 for tz in to_z for tx in to_x]
    along_zx = [
        pltpu.make_async_remote_copy(
            src_ref=second.at[to], dst_ref=second_in.at[k], send_sem=part_send.at[3 + k], recv_sem=part_recv.at[3 + k],
            device_id=(to * 4 + y, col), device_id_type=MESH,
        )
        for k, to in enumerate(lines[:-1])
    ]

    def turned(s):
        return acc[:, s * BS : (s + 1) * BS].T.astype(BF16)

    def scatter_first():
        for s in range(acc.shape[1] // BS):
            tile = turned(s).reshape(4, 4, 8, acc.shape[0])
            for to in range(4):
                first[to, 4 * s : 4 * s + 4] = tile[:, to]
        for copy in along_y:
            copy.start()

    def pass_first():
        for copy in along_y:
            copy.wait_recv()
        for half_of in range(2):
            some = pl.ds(half_of * 8, 8)
            total = first[y, some].astype(F32)
            for k in range(3):
                total = total + first_in[k, some].astype(F32)
            second[some] = total.astype(BF16)
        for copy in along_zx:
            copy.start()

    def scatter_second():
        for s in range(acc.shape[1] // BS):
            stage[s * 16 : (s + 1) * 16] = turned(s).reshape(16, 8, acc.shape[0])
        for slot, to in enumerate(owners):
            pltpu.make_async_remote_copy(
                src_ref=stage.at[to], dst_ref=land.at[slot], send_sem=sum_send, recv_sem=sum_recv,
                device_id=(to, col), device_id_type=MESH,
            ).start()

    all_sums = pltpu.make_async_remote_copy(
        src_ref=stage.at[pl.ds(0, nodes - 1)], dst_ref=land, send_sem=sum_send, recv_sem=sum_recv,
        device_id=across, device_id_type=MESH,
    )

    def write(total, half_at):
        at = pl.ds(pl.multiple_of(half_at * 2 * width, 2 * width), 2 * width)
        out[0, :, at] = total[:, : 2 * width]
        out[1, :, at] = total[:, 2 * width :]

    def land_all(copies):
        for copy in copies:
            copy.wait_recv()

    tell(0)

    loads[0].wait()
    own_body.wait_recv()
    fill(wi, xl, HB)
    for load in loads[1:5]:
        load.wait()
    products(wi, HB, nb // 2, HB)
    cross[0].wait_recv()
    pass_on[0].start()
    for copy in far_down:
        copy.start()
    cross[1].wait_recv()
    pass_on[1].start()
    for copy in far_up:
        copy.start()
    hear(0)
    tell(1)
    products(wi, nb // 2, nb - HB, HB)
    land_all(own_up)
    fill(we, xl, 0)
    products(we, 0, HB, 0)
    land_all(own_down)
    fill(wf, xl, nb - HB)
    products(wf, nb - HB, nb, nb - HB)
    cross[2].wait_recv()
    pass_on[2].start()
    loads[5].wait()
    project(0, nb, True)
    scatter_first()

    ends = [b - HB for b in INNER[1:-1]] + [nb]
    starts = [0] + ends[:-1]
    needs = (far_up + [pass_on[0], pass_on[2]], [pass_on[3]], [pass_on[4]], far_down + [pass_on[1], cross[5], cross_both])
    for p, (window, a, b) in enumerate(zip((w0, w1, w2, w3), starts, ends)):
        land_all(needs[p])
        fill(window, xr, a)
        products(window, a, b, a)
        project(a, b, p == 0)
        if p < 2:
            cross[3 + p].wait_recv()
            pass_on[3 + p].start()
        if p == 0:
            hear(1)
            pass_first()
    scatter_second()

    total = second[node // 4].astype(F32)
    for k, copy in enumerate(along_zx):
        copy.wait_recv()
        total = total + second_in[k].astype(F32)
    write(total, x_lo)
    all_sums.wait_recv()
    total = stage[node].astype(F32)
    for k in range(nodes - 1):
        total = total + land[k].astype(F32)
    write(total, 1 - x_lo)
    for copy in (*made, *along_y, *along_zx, all_sums):
        copy.wait_send()


def body(panel, basis, g_blocks, c_blocks, block_cols):
    nodes = lax.axis_size("node")
    nb = g_blocks.shape[0]
    width, states = panel.shape[1], basis.shape[1]
    ext = (nb + 2 * HB) * BS
    ends = [b - HB for b in INNER[1:-1]] + [nb]
    starts = [0] + ends[:-1]
    piece = (states // nodes, 4 * width)
    any_spec = pl.BlockSpec(memory_space=pl.ANY)
    vmem_spec = pl.BlockSpec(memory_space=pltpu.VMEM)
    windows = [(HB, nb - HB), (0, HB), (nb - HB, nb), *zip(starts, ends)]
    reduced = pl.pallas_call(
        functools.partial(kernel, nodes),
        out_shape=jax.ShapeDtypeStruct((2, *piece), F32),
        in_specs=[any_spec] * 4 + [pl.BlockSpec(memory_space=pltpu.SMEM)],
        out_specs=vmem_spec,
        scratch_shapes=[
            pltpu.VMEM((2 * width, ext), BF16),
            pltpu.VMEM((2 * width, ext), BF16),
            *[pltpu.VMEM((b - a + 2 * HB, 2 * width, BS), BF16) for a, b in windows],
            pltpu.VMEM(g_blocks.shape, BF16),
            pltpu.VMEM(c_blocks.shape, BF16),
            pltpu.VMEM(basis.shape, BF16),
            pltpu.VMEM((4 * width, nb * BS), BF16),
            pltpu.VMEM((4 * width, states), F32),
            pltpu.VMEM((nodes, *piece), BF16),
            pltpu.VMEM((nodes - 1, *piece), BF16),
            pltpu.VMEM((4, nodes // 4, *piece), BF16),
            pltpu.VMEM((3, nodes // 4, *piece), BF16),
            pltpu.VMEM((nodes // 4, *piece), BF16),
            pltpu.VMEM((nodes // 4 - 1, *piece), BF16),
            pltpu.SemaphoreType.DMA((6,)),
            pltpu.SemaphoreType.DMA((28,)),
            pltpu.SemaphoreType.DMA((28,)),
            pltpu.SemaphoreType.DMA,
            pltpu.SemaphoreType.DMA,
            pltpu.SemaphoreType.DMA((18,)),
            pltpu.SemaphoreType.DMA((18,)),
            pltpu.SemaphoreType.REGULAR((2,)),
        ],
        compiler_params=pltpu.CompilerParams(
            collective_id=0, has_side_effects=True, vmem_limit_bytes=55000 << 10
        ),
        name="project",
    )(panel.T, basis, g_blocks, c_blocks, block_cols.T)
    return reduced[0], reduced[1]


def solution(mesh):
    in_specs = (
        P("node", "col"),
        P("node", "col"),
        P("node", None, None, None),
        P("node", None, None, None),
        P("node", None),
    )
    out_specs = (P(("col", "node"), None), P(("col", "node"), None))
    return jax.shard_map(body, mesh=mesh, in_specs=in_specs, out_specs=out_specs, check_vma=False)
```

time: 47 us -> 45.5 us (0.968)
  Pallas kernels: 44.8 us -> 43 us
    pallas_call x1, Pallas kernels: 44.8 us -> 43 us  [body(): pl.pallas_call(functools.partial(kernel, nodes), out_shape=jax.ShapeDtype...]
    squeeze x1, local copies, waits for them, and re-layouts: 1.32 us -> 0.61 us  [body(): return (reduced[0], reduced[1])]
    unnamed x0 -> x2, local copies, waits for them, and re-layouts: none -> 0.67 us
where the time goes in v3:
time: 45.5 us; the launch traced here: 44.9 us
  Pallas kernels  43 us (95%)
  local copies, waits for them, and re-layouts  1.28 us (3%)
  between operations  0.65 us (1%)
    pallas_call x1, Pallas kernels, body(): pl.pallas_call(functools.partial(kernel, nodes), out_shape=jax.ShapeDtype...  43 us

profile of v3, /device:TPU:1, one launch (start us, length us, event | category | flops | bytes accessed | tf_op | source)
XLA Modules:
  0.0 44.9 jit_solution(9669301236874552937)
XLA Ops:
  0.6 0.0 copy-start
  0.6 0.7 %copy-done = s32[38,3]{0,1:T(4,128)S(1)} copy-done((s32[38,3]{0,1:T(4,128)S(1)}, s32[38,3]{0,1:T(4,128)}, u32[]{:S(2)}) %copy-start) | copy-done | bytes 480
  1.3 43.0 %project.1 = f32[2,8,256]{2,1,0:T(8,128)S(1)} custom-call(bf16[64,4864]{1,0:T(8,128)(2,1)} %bitcast.7, bf16[4864,512]{1,0:T(8,128)(2,1)} %basis.1, bf16[38,3,128,128]{3,2,1,0:T(8,128)(2,1)} %gb.1, bf16[38,3,128,128]{3,2,1,0:T(8,128)(2,1)} %cb.1, s32[3,38]{1,0:T(4,128)S(1)} %bitcast.6), custom_call_target="tpu_custom_call" | custom-call | tf_op jit(solution)/shard_map/project/pallas_call | solution.py:280
  44.3 0.6 %slice_bitcast_fusion = (f32[8,256]{1,0:T(8,128)}, f32[8,256]{1,0:T(8,128)}) fusion(f32[2,8,256]{2,1,0:T(8,128)S(1)} %project.1), kind=kLoop, calls=%fused_computation | loop fusion | bytes 32768 | tf_op jit(solution)/shard_map/squeeze | solution.py:314
Async XLA Ops:
  0.6 0.7 %copy-start = (s32[38,3]{0,1:T(4,128)S(1)}, s32[38,3]{0,1:T(4,128)}, u32[]{:S(2)}) copy-start(s32[38,3]{0,1:T(4,128)} %param.9) | copy-start | bytes 1372

commit v4 on v3

--- a/solution.py
+++ b/solution.py
@@ -20,9 +20,9 @@
 
 
 def kernel(
-    nodes, xt, basis, gb, cb, bc, out,
+    nodes, xt, basis, gb, cb, bc_any, out,
     xl, xr, wi, we, wf, w0, w1, w2, w3, gv, cv, bv, yt, acc,
-    stage, land, first, first_in, second, second_in, lsem, ssem, rsem, sum_send, sum_recv, part_send, part_recv, known,
+    stage, land, first, first_in, second, second_in, lsem, ssem, rsem, sum_send, sum_recv, part_send, part_recv, known, bc, bc_sem,
 ):
     nb = gb.shape[0]
     width = xt.shape[0]
@@ -45,6 +45,8 @@
             rows = pl.ds(part * half, half)
             loads.append(pltpu.make_async_copy(src.at[rows], dst.at[rows], lsem.at[1 + 2 * part + k]))
     loads.append(pltpu.make_async_copy(basis, bv, lsem.at[5]))
+    table = pltpu.make_async_copy(bc_any, bc, bc_sem)
+    table.start()
     for load in (loads[0], loads[1], loads[3], loads[2], loads[4], loads[5]):
         load.start()
 
@@ -212,6 +214,7 @@
     fill(wi, xl, HB)
     for load in loads[1:5]:
         load.wait()
+    table.wait()
     products(wi, HB, nb // 2, HB)
     cross[0].wait_recv()
     pass_on[0].start()
@@ -247,7 +250,7 @@
         if p < 2:
             cross[3 + p].wait_recv()
             pass_on[3 + p].start()
-        if p == 0:
+        if p == 1:
             hear(1)
             pass_first()
     scatter_second()
@@ -280,7 +283,7 @@
     reduced = pl.pallas_call(
         functools.partial(kernel, nodes),
         out_shape=jax.ShapeDtypeStruct((2, *piece), F32),
-        in_specs=[any_spec] * 4 + [pl.BlockSpec(memory_space=pltpu.SMEM)],
+        in_specs=[any_spec] * 5,
         out_specs=vmem_spec,
         scratch_shapes=[
             pltpu.VMEM((2 * width, ext), BF16),
@@ -305,6 +308,8 @@
             pltpu.SemaphoreType.DMA((18,)),
             pltpu.SemaphoreType.DMA((18,)),
             pltpu.SemaphoreType.REGULAR((2,)),
+            pltpu.SMEM(block_cols.shape[::-1], jnp.int32),
+            pltpu.SemaphoreType.DMA,
         ],
         compiler_params=pltpu.CompilerParams(
             collective_id=0, has_side_effects=True, vmem_limit_bytes=55000 << 10

time: 45.5 us -> 43.3 us (0.952)
  Pallas kernels: 43 us -> 40.9 us
    pallas_call x1, Pallas kernels: 43 us -> 40.9 us  [body(): pl.pallas_call(functools.partial(kernel, nodes), out_shape=jax.ShapeDtype...]
where the time goes in v4:
time: 43.3 us; the launch traced here: 42.8 us
  Pallas kernels  40.9 us (94%)
  local copies, waits for them, and re-layouts  1.28 us (3%)
  between operations  0.65 us (2%)
    pallas_call x1, Pallas kernels, body(): pl.pallas_call(functools.partial(kernel, nodes), out_shape=jax.ShapeDtype...  40.9 us

profile of v4, /device:TPU:1, one launch (start us, length us, event | category | flops | bytes accessed | tf_op | source)
XLA Modules:
  0.0 42.8 jit_solution(11517895969647288860)
XLA Ops:
  0.6 0.0 copy-start
  0.6 0.7 %copy-done = s32[38,3]{0,1:T(4,128)S(1)} copy-done((s32[38,3]{0,1:T(4,128)S(1)}, s32[38,3]{0,1:T(4,128)}, u32[]{:S(2)}) %copy-start) | copy-done | bytes 480
  1.3 40.9 %project.1 = f32[2,8,256]{2,1,0:T(8,128)S(1)} custom-call(bf16[64,4864]{1,0:T(8,128)(2,1)} %bitcast.7, bf16[4864,512]{1,0:T(8,128)(2,1)} %basis.1, bf16[38,3,128,128]{3,2,1,0:T(8,128)(2,1)} %gb.1, bf16[38,3,128,128]{3,2,1,0:T(8,128)(2,1)} %cb.1, s32[3,38]{1,0:T(4,128)S(1)} %bitcast.6), custom_call_target="tpu_custom_call" | custom-call | tf_op jit(solution)/shard_map/project/pallas_call | solution.py:283
  42.2 0.6 %slice_bitcast_fusion = (f32[8,256]{1,0:T(8,128)}, f32[8,256]{1,0:T(8,128)}) fusion(f32[2,8,256]{2,1,0:T(8,128)S(1)} %project.1), kind=kLoop, calls=%fused_computation | loop fusion | bytes 32768 | tf_op jit(solution)/shard_map/squeeze | solution.py:319
Async XLA Ops:
  0.6 0.7 %copy-start = (s32[38,3]{0,1:T(4,128)S(1)}, s32[38,3]{0,1:T(4,128)}, u32[]{:S(2)}) copy-start(s32[38,3]{0,1:T(4,128)} %param.9) | copy-start | bytes 1372

commit v5 on v4

--- a/solution.py
+++ b/solution.py
@@ -102,8 +102,8 @@
     for copy in (cross[0], cross[1], own_body, *own_up, *own_down, *cross[2:], cross_both):
         copy.start()
 
-    def fill(window, slices, shift):
-        for b in range(window.shape[0]):
+    def fill(window, slices, shift, blocks=None):
+        for b in range(window.shape[0]) if blocks is None else blocks:
             window[b] = slices[:, span(b + shift, b + shift + 1)]
 
     def products(window, first, last, shift):
@@ -241,10 +241,14 @@
 
     ends = [b - HB for b in INNER[1:-1]] + [nb]
     starts = [0] + ends[:-1]
-    needs = (far_up + [pass_on[0], pass_on[2]], [pass_on[3]], [pass_on[4]], far_down + [pass_on[1], cross[5], cross_both])
+    needs = (far_up + [pass_on[0], pass_on[2]], [pass_on[3]], [pass_on[4]], far_down + [pass_on[1]])
     for p, (window, a, b) in enumerate(zip((w0, w1, w2, w3), starts, ends)):
         land_all(needs[p])
-        fill(window, xr, a)
+        late = [k - a for k in range(INNER[-2] + HB, INNER[-1] + HB)] if p == 3 else []
+        fill(window, xr, a, [k for k in range(window.shape[0]) if k not in late])
+        if late:
+            land_all([cross[5], cross_both])
+            fill(window, xr, a, late)
         products(window, a, b, a)
         project(a, b, p == 0)
         if p < 2:

time: 43.3 us -> 43.3 us (level)
  no operation moved by 1% of the time
where the time goes in v5:
time: 43.3 us; the launch traced here: 42.8 us
  Pallas kernels  40.9 us (94%)
  local copies, waits for them, and re-layouts  1.28 us (3%)
  between operations  0.65 us (2%)
    pallas_call x1, Pallas kernels, body(): pl.pallas_call(functools.partial(kernel, nodes), out_shape=jax.ShapeDtype...  40.9 us

profile of v5, /device:TPU:1, one launch (start us, length us, event | category | flops | bytes accessed | tf_op | source)
XLA Modules:
  0.0 42.8 jit_solution(6118882885639734174)
XLA Ops:
  0.6 0.0 copy-start
  0.6 0.7 %copy-done = s32[38,3]{0,1:T(4,128)S(1)} copy-done((s32[38,3]{0,1:T(4,128)S(1)}, s32[38,3]{0,1:T(4,128)}, u32[]{:S(2)}) %copy-start) | copy-done | bytes 480
  1.3 40.9 %project.1 = f32[2,8,256]{2,1,0:T(8,128)S(1)} custom-call(bf16[64,4864]{1,0:T(8,128)(2,1)} %bitcast.7, bf16[4864,512]{1,0:T(8,128)(2,1)} %basis.1, bf16[38,3,128,128]{3,2,1,0:T(8,128)(2,1)} %gb.1, bf16[38,3,128,128]{3,2,1,0:T(8,128)(2,1)} %cb.1, s32[3,38]{1,0:T(4,128)S(1)} %bitcast.6), custom_call_target="tpu_custom_call" | custom-call | tf_op jit(solution)/shard_map/project/pallas_call | solution.py:287
  42.2 0.6 %slice_bitcast_fusion = (f32[8,256]{1,0:T(8,128)}, f32[8,256]{1,0:T(8,128)}) fusion(f32[2,8,256]{2,1,0:T(8,128)S(1)} %project.1), kind=kLoop, calls=%fused_computation | loop fusion | bytes 32768 | tf_op jit(solution)/shard_map/squeeze | solution.py:323
Async XLA Ops:
  0.6 0.7 %copy-start = (s32[38,3]{0,1:T(4,128)S(1)}, s32[38,3]{0,1:T(4,128)}, u32[]{:S(2)}) copy-start(s32[38,3]{0,1:T(4,128)} %param.9) | copy-start | bytes 1372
